TPU v7x, 32 devices: a whole 2x2x4 slice. The times are simulated.
32 devices in a mesh: feat: 4 (over y, x), label: 8 (over z, core).
Axes of the slice: x: 2, y: 2, z: 4, core: 2. Of those that a mesh axis runs over, the one named last changes fastest.
Arguments:
- documents: bfloat16 [160, 1024], P(None, 'label'), may hold values from -6 to 6
- expand_weight: bfloat16 [1024, 32768], P('label', 'feat'), may hold values from -0.1875 to 0.1875
- sparse_weight: bfloat16 [768, 16, 128, 128], P(('feat', 'label')), may hold values from -0.125 to 0.125
- feature_lists: int32 [768, 16], replicated, may hold values from 0 to 255, as said below
- positives: int32 [160, 8], replicated, may hold values from 0 to 98303
Outputs:
- grad_expand: bfloat16 [1024, 32768], P('label', 'feat')
- grad_sparse: bfloat16 [768, 16, 128, 128], P(('feat', 'label'))
Inputs may be any that keep to these rules, and one draw needn't show every extreme that they name: `feature_lists`: within each aligned group of 24 label blocks (taken in order), the entries name exactly 24 distinct feature blocks from each range of 64 consecutive blocks, each named exactly 4 times in the group; the 16 entries of one label block are distinct.
All inputs are finite; a program needn't handle non-finite values.
Results may differ from a plain program's by a relative error of at most 0.014.
Values may be sent and summed in bfloat16 or wider, within the bound.
No kernel may reach another device: no remote copies, remote signals or barrier semaphores. Data moves between devices by JAX's collectives and lax.ppermute only.
A program may use at most 192 MiB of HBM per device.

v0:
```python
import jax
import jax.numpy as jnp
from jax import lax
from jax.sharding import PartitionSpec as P

BLK = 128
FBLOCKS = 256
SLOTS = 16
LBLK_DEV = 24
CAP = 24


def on_device(documents, expand_weight, sparse_weight, feature_lists, positives):
    feat_count = lax.axis_size("feat")
    label_count = lax.axis_size("label")
    feat_index = lax.axis_index("feat")
    label_index = lax.axis_index("label")
    group = feat_index * label_count + label_index
    doc_count = documents.shape[0]
    width_local = expand_weight.shape[0]
    own_count = expand_weight.shape[1] // BLK
    local_weight = expand_weight.reshape(width_local, own_count, BLK)
    partial_pre = jnp.einsum(
        "dk,kbc->bdc", documents, local_weight, preferred_element_type=jnp.float32
    )
    summed_pre = lax.psum(partial_pre, "label")
    hidden = jnp.maximum(summed_pre, 0.0).astype(jnp.bfloat16)
    mine = lax.dynamic_slice_in_dim(feature_lists, group * LBLK_DEV, LBLK_DEV, 0)

    def sender_list(target):
        rows = lax.dynamic_slice_in_dim(
            feature_lists, (target * label_count + label_index) * LBLK_DEV, LBLK_DEV, 0
        )
        local_ids = feat_index * own_count + jnp.arange(own_count, dtype=jnp.int32)
        used = jnp.any(rows.reshape(-1)[:, None] == local_ids[None, :], axis=0)
        order = jnp.argsort(jnp.where(used, 0, 1).astype(jnp.int32), stable=True)
        return order[:CAP]

    send_index = jax.vmap(sender_list)(jnp.arange(feat_count, dtype=jnp.int32))
    outgoing = jnp.take(hidden, send_index, axis=0)
    incoming = lax.all_to_all(outgoing, "feat", split_axis=0, concat_axis=0, tiled=True)
    present = jnp.any(
        mine.reshape(-1)[:, None] == jnp.arange(FBLOCKS, dtype=jnp.int32)[None, :], axis=0
    )
    ranks = jnp.cumsum(present.reshape(feat_count, own_count).astype(jnp.int32), axis=1) - 1
    position_table = (jnp.arange(feat_count, dtype=jnp.int32)[:, None] * CAP + ranks).reshape(-1)
    slot_position = jnp.take(position_table, mine, axis=0)
    picked = jnp.take(incoming.reshape(feat_count * CAP, doc_count, BLK), slot_position, axis=0)
    logits = jnp.einsum("lsdc,lsce->dle", picked, sparse_weight, preferred_element_type=jnp.float32)
    label_ids = (group * LBLK_DEV + jnp.arange(LBLK_DEV, dtype=jnp.int32))[
        :, None
    ] * BLK + jnp.arange(BLK, dtype=jnp.int32)[None, :]
    targets = jnp.any(positives[:, :, None, None] == label_ids[None, None, :, :], axis=1).astype(
        jnp.float32
    )
    residual = (jax.nn.sigmoid(logits) - targets).astype(jnp.bfloat16)
    grad_sparse = jnp.einsum(
        "lsdc,dle->lsce", picked, residual, preferred_element_type=jnp.float32
    ).astype(jnp.bfloat16)
    back = jnp.einsum("dle,lsce->lsdc", residual, sparse_weight, preferred_element_type=jnp.float32)
    back_rows = back.reshape(LBLK_DEV * SLOTS, doc_count, BLK)
    group_part = jax.ops.segment_sum(
        back_rows, slot_position.reshape(-1), num_segments=feat_count * CAP
    )
    group_part = group_part.astype(jnp.bfloat16).reshape(feat_count, CAP, doc_count, BLK)
    returned = lax.all_to_all(group_part, "feat", split_axis=0, concat_axis=0, tiled=True)
    column_sum = jax.ops.segment_sum(
        returned.astype(jnp.float32).reshape(feat_count * CAP, doc_count, BLK),
        send_index.reshape(-1),
        num_segments=own_count,
    )
    block_grad = lax.psum(column_sum.astype(jnp.bfloat16), "label").astype(jnp.float32)
    grad_hidden = jnp.where(hidden > 0, block_grad, 0.0).astype(jnp.bfloat16)
    grad_expand = jnp.einsum(
        "dk,bdc->kbc", documents, grad_hidden, preferred_element_type=jnp.float32
    )
    grad_expand = grad_expand.reshape(width_local, own_count * BLK).astype(jnp.bfloat16)
    return (grad_expand, grad_sparse)


def solution(mesh):
    return jax.shard_map(
        on_device,
        mesh=mesh,
        in_specs=(
            P(None, "label"),
            P("label", "feat"),
            P(("feat", "label"), None, None, None),
            P(),
            P(),
        ),
        out_specs=(P("label", "feat"), P(("feat", "label"), None, None, None)),
        check_vma=False,
    )
```

profile of v0, /device:TPU:0, one launch (start us, length us, event | category | flops | bytes accessed | tf_op | source)
XLA Modules:
  0.0 502.6 jit_solution(14127657274373574968)
XLA Ops:
  7.2 8.1 %while.1 = (s32[]{:T(128)}, s32[768,16]{0,1:T(8,128)}, s32[4,2]{0,1:T(2,128)S(1)}, s32[4,24,16]{1,2,0:T(8,128)S(1)}, s32[]{:T(128)}) while((s32[]{:T(128)}, s32[768,16]{0,1:T(8,128)}, s32[4,2]{0,1:T(2,128)S(1)}, s32[4,24,16]{1,2,0:T(8,128)S(1)}, s32[]{:T(128)}) %tuple.25), condition=%wide.while_cond, body=%wide.while_body.sunk | while | flops 2 | bytes 9825 | solution.py:31
  17.1 4.0 convolution_bitcast_fusion
  21.1 111.1 %all-reduce.5 = bf16[64,160,128]{2,1,0:T(8,128)(2,1)} all-reduce(f32[64,160,128]{2,1,0:T(8,128)} %convolution_bitcast_fusion), channel_id=1, replica_groups=mesh['feat'=4,'label'=8] {'label'}, use_global_device_ids=true, to_apply=%region_0.0 | all-reduce | flops 1310720 | bytes 7864320 | tf_op jit(solution)/shard_map/psum | solution.py:26
  132.1 3.8 maximum_convert_fusion
  136.0 4.8 gather_fusion.1
  140.8 4.5 broadcast_select_fusion.5
  145.3 5.0 all-to-all-start
  155.3 3.7 compare_reduce_fusion
  159.0 32.3 %all-to-all-done = bf16[4,24,160,128]{3,2,1,0:T(8,128)(2,1)} async-done(((bf16[4,24,160,128]{3,2,1,0:T(8,128)(2,1)}), bf16[4,24,160,128]{3,2,1,0:T(8,128)(2,1)}, u32[]{:S(2)}, u32[]{:S(2)}) %all-to-all-start) | async-done | bytes 3932192 | tf_op jit(solution)/shard_map/all_to_all | solution.py:41
  191.3 14.7 %gather_fusion.2 = bf16[384,160,128]{2,1,0:T(8,128)(2,1)} fusion(bf16[96,160,128]{2,1,0:T(8,128)(2,1)} %bitcast.3, s32[1024]{0:T(1024)S(1)} %pad_clamp_fusion), kind=kCustom, calls=%fused_computation.2 | custom fusion | bytes 31458816 | tf_op jit(solution)/shard_map/jit(_take)/gather | solution.py:48
  206.0 11.4 %fusion.14 = bf16[160,24,128,1]{2,0,3,1:T(8,128)(2,1)S(1)} fusion(pred[160,24,128]{2,1,0:T(8,128)(4,1)S(1)} %compare_reduce_fusion, bf16[24,16,128,128]{3,2,1,0:T(8,128)(2,1)} %param.7, bf16[24,16,160,128]{3,2,1,0:T(8,128)(2,1)} %bitcast.62, pred[24,16]{1,0:T(8,128)(4,1)S(1)} %get-tuple-element.26), kind=kOutput, calls=%fused_computation.30 | convolution fusion | flops 2024079360 | bytes 29786496 | tf_op jit(solution)/shard_map/lsdc,lsce->dle/dot_general | solution.py:49
  217.4 15.2 %fusion.23 = f32[24,160,16,128]{3,1,2,0:T(8,128)} fusion(bf16[160,24,128,1]{2,0,3,1:T(8,128)(2,1)S(1)} %fusion.14, bf16[24,16,128,128]{3,2,1,0:T(8,128)(2,1)} %param.7), kind=kOutput, calls=%fused_computation.58 | convolution fusion | flops 2013265920 | bytes 45023232 | tf_op jit(solution)/shard_map/dle,lsce->lsdc/dot_general | solution.py:60
  232.6 4.2 broadcast_in_dim.58
  236.8 87.4 %scatter_fusion = f32[96,160,128]{2,1,0:T(8,128)} fusion(f32[96,160,128]{2,1,0:T(8,128)} %broadcast_in_dim.58, s32[384]{0:T(512)S(1)} %reshape.186, f32[384,160,128]{2,1,0:T(8,128)} %bitcast.61), kind=kCustom, calls=%fused_computation.3 | custom fusion | flops 7864320 | bytes 94373376 | tf_op jit(solution)/shard_map/scatter-add | solution.py:62
  324.3 5.8 %convert_element_type.45 = bf16[96,160,128]{2,1,0:T(8,128)(2,1)} convert(f32[96,160,128]{2,1,0:T(8,128)} %scatter_fusion) | non-fusion elementwise | flops 1966080 | bytes 11796480 | tf_op jit(solution)/shard_map/convert_element_type | solution.py:65
  330.1 4.8 all-to-all-start.1
  335.4 43.7 %all-to-all-done.1 = bf16[4,24,160,128]{3,2,1,0:T(8,128)(2,1)} async-done(((bf16[4,24,160,128]{3,2,1,0:T(8,128)(2,1)}), bf16[4,24,160,128]{3,2,1,0:T(8,128)(2,1)}, u32[]{:S(2)}, u32[]{:S(2)}) %all-to-all-start.1) | async-done | bytes 3932192 | tf_op jit(solution)/shard_map/all_to_all | solution.py:66
  379.1 6.4 %bitcast_convert_fusion = f32[96,160,128]{2,1,0:T(8,128)} fusion(bf16[4,24,160,128]{3,2,1,0:T(8,128)(2,1)} %all-to-all-done.1), kind=kLoop, calls=%fused_computation.16 | loop fusion | flops 1966080 | bytes 11796480 | tf_op jit(solution)/shard_map/reshape | solution.py:68
  388.4 22.5 %scatter_fusion.1 = f32[64,160,128]{2,1,0:T(8,128)} fusion(f32[64,160,128]{2,1,0:T(8,128)} %broadcast.134, s32[96]{0:T(128)S(1)} %reshape.194, f32[96,160,128]{2,1,0:T(8,128)} %bitcast_convert_fusion), kind=kCustom, calls=%fused_computation.4 | custom fusion | flops 1966080 | bytes 23593344 | tf_op jit(solution)/shard_map/scatter-add | solution.py:67
  411.0 4.4 convert_element_type.46
  415.4 14.3 %fusion.4 = bf16[24,16,128,128]{3,2,1,0:T(8,128)(2,1)} fusion(bf16[160,24,128,1]{2,0,3,1:T(8,128)(2,1)S(1)} %fusion.14, bf16[24,16,160,128]{3,2,1,0:T(8,128)(2,1)} %bitcast.63, pred[24,16]{1,0:T(8,128)(4,1)S(1)} %get-tuple-element.26), kind=kOutput, calls=%fused_computation.13 | convolution fusion | flops 2027421696 | bytes 29294976 | tf_op jit(solution)/shard_map/lsdc,dle->lsce/dot_general | solution.py:57
  429.6 56.8 %all-reduce.4.cloned.1.call-done = bf16[64,160,128]{2,1,0:T(8,128)(2,1)} async-done(((bf16[64,160,128]{2,1,0:T(8,128)(2,1)}), bf16[64,160,128]{2,1,0:T(8,128)(2,1)}) %all-reduce.4.cloned.1.call-update) | async-done | bytes 2621456 | tf_op jit(solution)/shard_map/psum | solution.py:72
  486.5 5.2 %fusion.13 = bf16[64,128,128]{2,1,0:T(8,128)(2,1)} fusion(bf16[64,160,128]{2,1,0:T(8,128)(2,1)} %all-reduce.4.cloned.1.call-done, bf16[160,128]{1,0:T(8,128)(2,1)S(1)} %copy-done.2, bf16[64,160,128]{2,1,0:T(8,128)(2,1)} %all-reduce.5), kind=kOutput, calls=%fused_computation.29 | convolution fusion | flops 345767936 | bytes 7380992 | tf_op jit(solution)/shard_map/dk,bdc->kbc/dot_general | solution.py:74
  491.6 4.1 copy.28
  (65 shorter events, 18.3 us)
Async XLA Ops:
  7.2 9.9 %copy-start = (bf16[128,8192]{1,0:T(8,128)(2,1)S(1)}, bf16[128,8192]{1,0:T(8,128)(2,1)}, u32[]{:S(2)}) copy-start(bf16[128,8192]{1,0:T(8,128)(2,1)} %param.6) | copy-start | bytes 6291460
  145.3 46.0 %all-to-all-start = ((bf16[4,24,160,128]{3,2,1,0:T(8,128)(2,1)}), bf16[4,24,160,128]{3,2,1,0:T(8,128)(2,1)}, u32[]{:S(2)}, u32[]{:S(2)}) async-start(bf16[4,24,160,128]{3,2,1,0:T(8,128)(2,1)} %broadcast_select_fusion.5), calls=%async_computation | async-start | bytes 7864320 | tf_op jit(solution)/shard_map/all_to_all | solution.py:41
  152.0 3.1 copy-start.3
  330.1 48.9 %all-to-all-start.1 = ((bf16[4,24,160,128]{3,2,1,0:T(8,128)(2,1)}), bf16[4,24,160,128]{3,2,1,0:T(8,128)(2,1)}, u32[]{:S(2)}, u32[]{:S(2)}) async-start(bf16[4,24,160,128]{3,2,1,0:T(8,128)(2,1)} %bitcast.64), calls=%async_computation.1 | async-start | bytes 7864320 | tf_op jit(solution)/shard_map/all_to_all | solution.py:66
  334.9 151.5 %all-reduce.4.cloned.1.call-start = ((), (), s32[]{:S(2)}) async-start(), calls=%async_computation.2 | async-start | bytes 5242880 | tf_op jit(solution)/shard_map/psum | solution.py:72
  415.3 71.1 %copy-start.2 = (bf16[160,128]{1,0:T(8,128)(2,1)S(1)}, bf16[160,128]{1,0:T(8,128)(2,1)}, u32[]{:S(2)}) copy-start(bf16[160,128]{1,0:T(8,128)(2,1)} %param.5) | copy-start | bytes 122884
  415.4 80.4 %copy-start.1 = (bf16[128,8192]{1,0:T(8,128)(2,1)S(1)}, bf16[128,8192]{1,0:T(8,128)(2,1)}, u32[]{:S(2)}) copy-start(bf16[128,8192]{1,0:T(8,128)(2,1)} %param.6) | copy-start | bytes 6291460
Sparse Core Ops, SparseCore 0:
  415.5 70.9 all-reduce.3
where the time goes:
time: 505 us; the launch traced here: 503 us
  other arithmetic  140 us (28%)
  waiting for transfers between devices  133 us (26%)
  blocking collectives  111 us (22%)
  matrix products  50.1 us (10%)
  local copies, waits for them, and re-layouts  44 us (9%)
  between operations  14.2 us (3%)
  starting transfers between devices  10 us (2%)
    psum x1, blocking collectives, on_device(): summed_pre = lax.psum(partial_pre, 'label')  111 us
    scatter-add x1, other arithmetic, on_device(): jax.ops.segment_sum(back_rows, slot_position.reshape(-1), num_segments=fe...  87.4 us
    psum x1, waiting for transfers between devices, on_device(): lax.psum(column_sum.astype(jnp.bfloat16), 'label').astype(jnp.float32)  56.8 us
    all_to_all x1, waiting for transfers between devices, on_device(): lax.all_to_all(group_part, 'feat', split_axis=0, concat_axis=0, tiled=True)  43.7 us
    all_to_all x1, waiting for transfers between devices, on_device(): lax.all_to_all(outgoing, 'feat', split_axis=0, concat_axis=0, tiled=True)  32.3 us
    scatter-add x1, other arithmetic, on_device(): jax.ops.segment_sum(returned.astype(jnp.float32).reshape(feat_count * CAP...  22.5 us
    dot_general x1, matrix products, on_device(): jnp.einsum('dle,lsce->lsdc', residual, sparse_weight, preferred_element_t...  15.2 us
    gather x1, local copies, waits for them, and re-layouts, on_device(): jnp.take(incoming.reshape(feat_count * CAP, doc_count, BLK), slot_positio...  14.7 us
  transfers between devices with their start and end apart: 3, of which 3 were waited for; matrix products, arithmetic and copies ran while one was open for 5% of the time, Pallas kernels for 0%

commit v1 on v0

--- a/solution.py
+++ b/solution.py
@@ -23,7 +23,11 @@
     partial_pre = jnp.einsum(
         "dk,kbc->bdc", documents, local_weight, preferred_element_type=jnp.float32
     )
-    summed_pre = lax.psum(partial_pre, "label")
+    summed_pre = partial_pre
+    for hop in (1, 2, 4):
+        summed_pre = summed_pre + lax.ppermute(
+            summed_pre, "label", [(dev, dev ^ hop) for dev in range(8)]
+        )
     hidden = jnp.maximum(summed_pre, 0.0).astype(jnp.bfloat16)
     mine = lax.dynamic_slice_in_dim(feature_lists, group * LBLK_DEV, LBLK_DEV, 0)
 

time: 505 us -> 745 us (1.48)
  waiting for transfers between devices: 133 us -> 472 us
  blocking collectives: 111 us -> 0 us
    ppermute x0 -> x3, waiting for transfers between devices: none -> 337 us  [on_device(): lax.ppermute(summed_pre, 'label', [(dev, dev ^ hop) for dev in range(8)])]
    psum x1 -> x0, blocking collectives: 111 us -> none  [on_device(): summed_pre = lax.psum(partial_pre, 'label')]
  transfers between devices with their start and end apart: 3 -> 6, of which waited for: 3 -> 6; matrix products, arithmetic and copies ran while one was open for 5% -> 4% of each run, Pallas kernels for 0% -> 0%
where the time goes in v1:
time: 745 us; the launch traced here: 743 us
  waiting for transfers between devices  472 us (63%)
  other arithmetic  147 us (20%)
  matrix products  47.7 us (6%)
  local copies, waits for them, and re-layouts  45.6 us (6%)
  starting transfers between devices  16.3 us (2%)
  between operations  14.2 us (2%)
    ppermute x3, waiting for transfers between devices, on_device(): lax.ppermute(summed_pre, 'label', [(dev, dev ^ hop) for dev in range(8)])  337 us
    scatter-add x1, other arithmetic, on_device(): jax.ops.segment_sum(back_rows, slot_position.reshape(-1), num_segments=fe...  87.4 us
    psum x1, waiting for transfers between devices, on_device(): lax.psum(column_sum.astype(jnp.bfloat16), 'label').astype(jnp.float32)  55.8 us
    all_to_all x1, waiting for transfers between devices, on_device(): lax.all_to_all(group_part, 'feat', split_axis=0, concat_axis=0, tiled=True)  43.7 us
    all_to_all x1, waiting for transfers between devices, on_device(): lax.all_to_all(outgoing, 'feat', split_axis=0, concat_axis=0, tiled=True)  35.3 us
    scatter-add x1, other arithmetic, on_device(): jax.ops.segment_sum(returned.astype(jnp.float32).reshape(feat_count * CAP...  22.5 us
    dot_general x1, matrix products, on_device(): jnp.einsum('dle,lsce->lsdc', residual, sparse_weight, preferred_element_t...  15.2 us
  transfers between devices with their start and end apart: 6, of which 6 were waited for; matrix products, arithmetic and copies ran while one was open for 4% of the time, Pallas kernels for 0%

profile of v1, /device:TPU:0, one launch (start us, length us, event | category | flops | bytes accessed | tf_op | source)
XLA Modules:
  0.0 743.0 jit_solution(711692055217231544)
XLA Ops:
  10.9 8.3 %collective-permute-done = f32[64,160,128]{2,1,0:T(8,128)S(1)} collective-permute-done((f32[64,160,128]{2,1,0:T(8,128)S(1)}, f32[64,160,128]{2,1,0:T(8,128)S(1)}, u32[]{:S(2)}, u32[]{:S(2)}) %collective-permute-start) | collective-permute-done | bytes 5242912 | tf_op jit(solution)/shard_map/ppermute | solution.py:28
  23.2 113.3 %collective-permute-done.1 = f32[64,160,128]{2,1,0:T(8,128)S(1)} collective-permute-done((f32[64,160,128]{2,1,0:T(8,128)S(1)}, f32[64,160,128]{2,1,0:T(8,128)S(1)}, u32[]{:S(2)}, u32[]{:S(2)}) %collective-permute-start.1) | collective-permute-done | bytes 5242912 | tf_op jit(solution)/shard_map/ppermute | solution.py:28
  142.6 8.2 %while.1 = (s32[]{:T(128)}, s32[768,16]{0,1:T(8,128)}, s32[4,2]{0,1:T(2,128)S(1)}, s32[4,24,16]{1,2,0:T(8,128)S(1)}, s32[]{:T(128)}) while((s32[]{:T(128)}, s32[768,16]{0,1:T(8,128)}, s32[4,2]{0,1:T(2,128)S(1)}, s32[4,24,16]{1,2,0:T(8,128)S(1)}, s32[]{:T(128)}) %tuple.25), condition=%wide.while_cond, body=%wide.while_body.sunk | while | flops 2 | bytes 9825 | solution.py:35
  152.6 215.3 %collective-permute-done.2 = f32[64,160,128]{2,1,0:T(8,128)} collective-permute-done((f32[64,160,128]{2,1,0:T(8,128)}, f32[64,160,128]{2,1,0:T(8,128)}, u32[]{:S(2)}, u32[]{:S(2)}) %collective-permute-start.2) | collective-permute-done | bytes 5242912 | tf_op jit(solution)/shard_map/ppermute | solution.py:28
  367.9 6.6 maximum_convert_fusion
  374.4 4.8 gather_fusion.1
  379.3 4.5 broadcast_select_fusion.5
  383.7 5.0 all-to-all-start
  397.4 35.3 %all-to-all-done = bf16[4,24,160,128]{3,2,1,0:T(8,128)(2,1)} async-done(((bf16[4,24,160,128]{3,2,1,0:T(8,128)(2,1)}), bf16[4,24,160,128]{3,2,1,0:T(8,128)(2,1)}, u32[]{:S(2)}, u32[]{:S(2)}) %all-to-all-start) | async-done | bytes 3932192 | tf_op jit(solution)/shard_map/all_to_all | solution.py:45
  432.7 14.7 %gather_fusion.2 = bf16[384,160,128]{2,1,0:T(8,128)(2,1)} fusion(bf16[96,160,128]{2,1,0:T(8,128)(2,1)} %bitcast.3, s32[1024]{0:T(1024)S(1)} %pad_clamp_fusion), kind=kCustom, calls=%fused_computation.2 | custom fusion | bytes 31458816 | tf_op jit(solution)/shard_map/jit(_take)/gather | solution.py:52
  447.4 11.4 %fusion.14 = bf16[160,24,128,1]{2,0,3,1:T(8,128)(2,1)S(1)} fusion(pred[160,24,128]{2,1,0:T(8,128)(4,1)S(1)} %compare_reduce_fusion, bf16[24,16,128,128]{3,2,1,0:T(8,128)(2,1)} %param.7, bf16[24,16,160,128]{3,2,1,0:T(8,128)(2,1)} %bitcast.62, pred[24,16]{1,0:T(8,128)(4,1)S(1)} %get-tuple-element.26), kind=kOutput, calls=%fused_computation.30 | convolution fusion | flops 2024079360 | bytes 29786496 | tf_op jit(solution)/shard_map/lsdc,lsce->dle/dot_general | solution.py:53
  458.9 15.2 %fusion.23 = f32[24,160,16,128]{3,1,2,0:T(8,128)} fusion(bf16[160,24,128,1]{2,0,3,1:T(8,128)(2,1)S(1)} %fusion.14, bf16[24,16,128,128]{3,2,1,0:T(8,128)(2,1)} %param.7), kind=kOutput, calls=%fused_computation.58 | convolution fusion | flops 2013265920 | bytes 45023232 | tf_op jit(solution)/shard_map/dle,lsce->lsdc/dot_general | solution.py:64
  474.1 4.2 broadcast_in_dim.58
  478.3 87.4 %scatter_fusion = f32[96,160,128]{2,1,0:T(8,128)} fusion(f32[96,160,128]{2,1,0:T(8,128)} %broadcast_in_dim.58, s32[384]{0:T(512)S(1)} %reshape.186, f32[384,160,128]{2,1,0:T(8,128)} %bitcast.61), kind=kCustom, calls=%fused_computation.3 | custom fusion | flops 7864320 | bytes 94373376 | tf_op jit(solution)/shard_map/scatter-add | solution.py:66
  565.7 5.8 convert_element_type.45
  571.6 4.8 all-to-all-start.1
  576.8 43.7 %all-to-all-done.1 = bf16[4,24,160,128]{3,2,1,0:T(8,128)(2,1)} async-done(((bf16[4,24,160,128]{3,2,1,0:T(8,128)(2,1)}), bf16[4,24,160,128]{3,2,1,0:T(8,128)(2,1)}, u32[]{:S(2)}, u32[]{:S(2)}) %all-to-all-start.1) | async-done | bytes 3932192 | tf_op jit(solution)/shard_map/all_to_all | solution.py:70
  620.5 6.4 bitcast_convert_fusion
  629.9 22.5 %scatter_fusion.1 = f32[64,160,128]{2,1,0:T(8,128)} fusion(f32[64,160,128]{2,1,0:T(8,128)} %broadcast.134, s32[96]{0:T(128)S(1)} %reshape.194, f32[96,160,128]{2,1,0:T(8,128)} %bitcast_convert_fusion), kind=kCustom, calls=%fused_computation.4 | custom fusion | flops 1966080 | bytes 23593344 | tf_op jit(solution)/shard_map/scatter-add | solution.py:71
  652.4 4.4 convert_element_type.46
  656.8 14.3 %fusion.4 = bf16[24,16,128,128]{3,2,1,0:T(8,128)(2,1)} fusion(bf16[160,24,128,1]{2,0,3,1:T(8,128)(2,1)S(1)} %fusion.14, bf16[24,16,160,128]{3,2,1,0:T(8,128)(2,1)} %bitcast.63, pred[24,16]{1,0:T(8,128)(4,1)S(1)} %get-tuple-element.26), kind=kOutput, calls=%fused_computation.13 | convolution fusion | flops 2027421696 | bytes 29294976 | tf_op jit(solution)/shard_map/lsdc,dle->lsce/dot_general | solution.py:61
  671.1 55.8 %all-reduce.3.cloned.1.call-done = bf16[64,160,128]{2,1,0:T(8,128)(2,1)} async-done(((bf16[64,160,128]{2,1,0:T(8,128)(2,1)}), bf16[64,160,128]{2,1,0:T(8,128)(2,1)}) %all-reduce.3.cloned.1.call-update) | async-done | bytes 2621456 | tf_op jit(solution)/shard_map/psum | solution.py:76
  726.9 5.2 fusion.13
  732.0 4.1 copy.28
  (72 shorter events, 35.8 us)
Async XLA Ops:
  7.2 1.6 copy-start
  10.4 8.8 %collective-permute-start = (f32[64,160,128]{2,1,0:T(8,128)S(1)}, f32[64,160,128]{2,1,0:T(8,128)S(1)}, u32[]{:S(2)}, u32[]{:S(2)}) collective-permute-start(f32[64,160,128]{2,1,0:T(8,128)S(1)} %convolution_bitcast_fusion), channel_id=1, source_target_pairs={{0,1},{1,0},{2,3},{3,2},{4,5},{5,4},{6,7},{7,6},{8,9},{9,8},{10,11... | collective-permute-start | bytes 15728648 | tf_op jit(solution)/shard_map/ppermute | solution.py:28
  20.2 116.3 %collective-permute-start.1 = (f32[64,160,128]{2,1,0:T(8,128)S(1)}, f32[64,160,128]{2,1,0:T(8,128)S(1)}, u32[]{:S(2)}, u32[]{:S(2)}) collective-permute-start(f32[64,160,128]{2,1,0:T(8,128)S(1)} %add.130), channel_id=1, source_target_pairs={{0,2},{1,3},{2,0},{3,1},{4,6},{5,7},{6,4},{7,5},{8,10},{9,11},{10,... | collective-permute-start | bytes 15728648 | tf_op jit(solution)/shard_map/ppermute | solution.py:28
  139.8 228.1 %collective-permute-start.2 = (f32[64,160,128]{2,1,0:T(8,128)}, f32[64,160,128]{2,1,0:T(8,128)}, u32[]{:S(2)}, u32[]{:S(2)}) collective-permute-start(f32[64,160,128]{2,1,0:T(8,128)} %add.131), channel_id=1, source_target_pairs={{0,4},{1,5},{2,6},{3,7},{4,0},{5,1},{6,2},{7,3},{8,12},{9,13},{10,... | collective-permute-start | bytes 15728648 | tf_op jit(solution)/shard_map/ppermute | solution.py:28
  383.7 49.0 %all-to-all-start = ((bf16[4,24,160,128]{3,2,1,0:T(8,128)(2,1)}), bf16[4,24,160,128]{3,2,1,0:T(8,128)(2,1)}, u32[]{:S(2)}, u32[]{:S(2)}) async-start(bf16[4,24,160,128]{3,2,1,0:T(8,128)(2,1)} %broadcast_select_fusion.5), calls=%async_computation | async-start | bytes 7864320 | tf_op jit(solution)/shard_map/all_to_all | solution.py:45
  390.4 3.1 copy-start.3
  571.6 48.9 %all-to-all-start.1 = ((bf16[4,24,160,128]{3,2,1,0:T(8,128)(2,1)}), bf16[4,24,160,128]{3,2,1,0:T(8,128)(2,1)}, u32[]{:S(2)}, u32[]{:S(2)}) async-start(bf16[4,24,160,128]{3,2,1,0:T(8,128)(2,1)} %bitcast.64), calls=%async_computation.1 | async-start | bytes 7864320 | tf_op jit(solution)/shard_map/all_to_all | solution.py:70
  576.4 150.5 %all-reduce.3.cloned.1.call-start = ((), (), s32[]{:S(2)}) async-start(), calls=%async_computation.2 | async-start | bytes 5242880 | tf_op jit(solution)/shard_map/psum | solution.py:76
  656.8 70.1 %copy-start.2 = (bf16[160,128]{1,0:T(8,128)(2,1)S(1)}, bf16[160,128]{1,0:T(8,128)(2,1)}, u32[]{:S(2)}) copy-start(bf16[160,128]{1,0:T(8,128)(2,1)} %param.5) | copy-start | bytes 122884
  656.8 79.3 %copy-start.1 = (bf16[128,8192]{1,0:T(8,128)(2,1)S(1)}, bf16[128,8192]{1,0:T(8,128)(2,1)}, u32[]{:S(2)}) copy-start(bf16[128,8192]{1,0:T(8,128)(2,1)} %param.6) | copy-start | bytes 6291460
Sparse Core Ops, SparseCore 0:
  656.9 69.8 all-reduce.2
